TPU v7x, 32 devices: a whole 2x2x4 slice. The times are simulated.
32 devices in a mesh: parts: 2 (over y), slab: 4 (over z), blk: 2 (over x), head: 2 (over core).
Axes of the slice: x: 2, y: 2, z: 4, core: 2. Of those that a mesh axis runs over, the one named last changes fastest.
Arguments:
- features: bfloat16 [4096, 512], P(('parts', 'slab', 'blk')), parts along dimension 0, may hold values from -16 to 16
- cotangent: bfloat16 [4096, 512], P(('parts', 'slab', 'blk')), parts along dimension 0, may hold values from -6 to 6
- w_query: bfloat16 [512, 512], P(None, 'head'), may hold values from -0.25 to 0.25
- w_key: bfloat16 [512, 512], P(None, 'head'), may hold values from -0.25 to 0.25
- w_value: bfloat16 [512, 512], P(None, 'head'), may hold values from -0.25 to 0.25
- w_out: bfloat16 [512, 512], P('head'), may hold values from -0.25 to 0.25
- adjacency: int32 [32, 3], P(('parts', 'slab', 'blk')), parts along dimension 0, may hold values from 0 to 1, as said below
- partner: int32 [3, 32], P(None, ('parts', 'slab', 'blk')), parts along dimension 1, may hold values from 0 to 15, as said below
- node_order: int32 [4096], P(('parts', 'slab', 'blk')), parts along dimension 0, may hold values from 0 to 255, as said below
Outputs:
- grad_input: bfloat16 [4096, 512], P(('parts', 'slab', 'blk'), 'head'), parts along dimension 0
There are 2 independent parts, one for each index of `parts`. A program takes and returns all parts, laid end to end along the dimension named above; an argument that names none is the same for every part. Nothing has to cross between parts.
Inputs may be any that keep to these rules, and one draw needn't show every extreme that they name: `adjacency`: column 1 (the block itself) is always 1. partner[m, g] is the block at the same position among its device's 2 blocks, on the device of the same blk index in another slab; partner[m, partner[m, g]] = g. Of the 3 * 2 (matching, block) pairs of one device, at most 2 have their partner in one slab, and on every device exactly 2 do for some slab. `node_order`: within each device's 2 * 128 positions, a permutation of the device's rows.
All inputs are finite; a program needn't handle non-finite values.
Results may differ from a plain program's by a relative error of at most 0.013.
The roundings to bfloat16 on the way count: a program that leaves them out, or rounds other values in their place, can miss the bound.
Values may be sent and summed in bfloat16 or wider, within the bound.
A program may use at most 64 MiB of HBM per device.

v0:
```python
import jax
import jax.numpy as jnp
from jax import lax
from jax.sharding import PartitionSpec as P

HEAD_DIM = 64


def padded_2(shard, sides, width):
    for axis, dim in sides:
        count, length = (lax.axis_size(axis), shard.shape[dim])
        up = [(i, (i + 1) % count) for i in range(count)]
        down = [(j, i) for i, j in up]
        last = lax.slice_in_dim(shard, length - width, length, axis=dim)
        first = lax.slice_in_dim(shard, 0, width, axis=dim)
        before = lax.ppermute(last, axis, up)
        after = lax.ppermute(first, axis, down)
        shard = jnp.concatenate([before, shard, after], axis=dim)
    return shard


def from_behind(value, axis, steps):
    count = lax.axis_size(axis)
    pairs = [(source, (source + steps) % count) for source in range(count)]
    return lax.ppermute(value, axis, pairs)


def attend(queries, grad_rows, key_rows, values, switch, score_scale):
    block_len = queries.shape[1]
    scores = (
        jnp.einsum("gqhd,gkhd->ghqk", queries, key_rows, preferred_element_type=jnp.float32)
        * score_scale
    )
    keys_on = jnp.repeat(switch, block_len, axis=1)
    scores = jnp.where(keys_on[:, None, None, :], scores, -jnp.inf)
    row_peak = jnp.max(scores, axis=-1, keepdims=True)
    row_total = jnp.log(jnp.sum(jnp.exp(scores - row_peak), axis=-1, keepdims=True)) + row_peak
    attention = jnp.exp(scores - row_total)
    attention_low = attention.astype(jnp.bfloat16)
    mixed_rows = jnp.einsum(
        "ghqk,gkhd->gqhd", attention_low, values, preferred_element_type=jnp.float32
    )
    row_dot = jnp.transpose(jnp.sum(grad_rows.astype(jnp.float32) * mixed_rows, axis=-1), (0, 2, 1))
    grad_attention = jnp.einsum(
        "gqhd,gkhd->ghqk", grad_rows, values, preferred_element_type=jnp.float32
    )
    grad_scores = (attention * (grad_attention - row_dot[..., None])).astype(jnp.bfloat16)
    grad_query = score_scale * jnp.einsum(
        "ghqk,gkhd->gqhd", grad_scores, key_rows, preferred_element_type=jnp.float32
    )
    grad_key = score_scale * jnp.einsum(
        "ghqk,gqhd->gkhd", grad_scores, queries, preferred_element_type=jnp.float32
    )
    grad_value = jnp.einsum(
        "ghqk,gqhd->gkhd", attention_low, grad_rows, preferred_element_type=jnp.float32
    )
    return (grad_query, grad_key, grad_value, row_total[..., 0], row_dot)


def to_slots(stacked, slot_block, block_count):
    blocked = stacked.reshape((stacked.shape[0], block_count, -1) + stacked.shape[2:])
    padded = jnp.concatenate([blocked, jnp.zeros_like(blocked[:, :1])], axis=1)
    return jnp.take(padded, slot_block, axis=1)


def body(features, cotangent, w_query, w_key, w_value, w_out, adjacency, partner, node_order):
    rows_dev = features.shape[0]
    block_count = adjacency.shape[0]
    block_len = rows_dev // block_count
    feat_width = w_query.shape[1]
    head_count = feat_width // HEAD_DIM
    score_scale = HEAD_DIM ** (-0.5)
    slab_count = lax.axis_size("slab")
    cycle_len = lax.axis_size("blk") * block_count
    capacity = max(1, (3 * block_count + slab_count - 2) // (slab_count - 1))
    slot_count = slab_count * capacity
    item_count = 3 * block_count
    inputs = jnp.take(features, node_order, axis=0)
    upstream = jnp.take(cotangent, node_order, axis=0)
    query_rows = jnp.dot(inputs, w_query, preferred_element_type=jnp.float32).astype(jnp.bfloat16)
    key_rows = jnp.dot(inputs, w_key, preferred_element_type=jnp.float32).astype(jnp.bfloat16)
    value_rows = jnp.dot(inputs, w_value, preferred_element_type=jnp.float32).astype(jnp.bfloat16)
    contract = (((1,), (1,)), ((), ()))
    grad_mix = lax.dot_general(
        upstream, w_out, contract, preferred_element_type=jnp.float32
    ).astype(jnp.bfloat16)
    pair_rows = jnp.stack([key_rows, value_rows])
    item_dest = (partner // cycle_len).reshape(-1)
    order_ids = jnp.arange(item_count, dtype=jnp.int32)
    earlier = order_ids[None, :] < order_ids[:, None]
    same_dest = item_dest[None, :] == item_dest[:, None]
    item_rank = jnp.sum((earlier & same_dest).astype(jnp.int32), axis=1)
    item_slot = item_dest * capacity + item_rank
    slot_ids = jnp.arange(slot_count, dtype=jnp.int32)
    slot_hit = (item_slot[None, :] == slot_ids[:, None]).astype(jnp.int32)
    slot_used = jnp.sum(slot_hit, axis=1)
    slot_item = jnp.sum(slot_hit * order_ids[None, :], axis=1) + (1 - slot_used) * item_count
    slot_block = jnp.where(slot_used > 0, slot_item % block_count, block_count)
    widened = padded_2(pair_rows, (("blk", 1),), block_len)
    widened = widened.reshape(2, block_count + 2, block_len, feat_width)
    near_rows = jnp.stack(
        [widened[:, offset : offset + block_count] for offset in range(3)], axis=2
    )
    sent_slots = to_slots(pair_rows, slot_block, block_count)
    arrived = lax.all_to_all(sent_slots, "slab", split_axis=1, concat_axis=1, tiled=True)
    far_rows = jnp.take(arrived, item_slot, axis=1)
    far_rows = far_rows.reshape(2, 3, block_count, block_len, feat_width)
    far_rows = jnp.transpose(far_rows, (0, 2, 1, 3, 4))
    gathered = jnp.concatenate([near_rows, far_rows], axis=2)
    gathered = gathered.reshape(2, block_count, 6 * block_len, head_count, HEAD_DIM)
    switch = jnp.concatenate([adjacency > 0, jnp.ones((block_count, 3), dtype=bool)], axis=1)
    query_blocks = query_rows.reshape(block_count, block_len, head_count, HEAD_DIM)
    grad_blocks = grad_mix.reshape(block_count, block_len, head_count, HEAD_DIM)

    def halves(source):
        return source.reshape((2, block_count // 2) + source.shape[1:])

    def visit_half(pieces):
        return attend(pieces[0], pieces[1], pieces[2], pieces[3], pieces[4], score_scale)

    results = lax.map(
        visit_half,
        (
            halves(query_blocks),
            halves(grad_blocks),
            halves(gathered[0]),
            halves(gathered[1]),
            halves(switch),
        ),
    )
    merged = [output.reshape((block_count,) + output.shape[2:]) for output in results]
    grad_query, grad_key, grad_value, row_total, row_dot = merged
    key_grads = jnp.stack([grad_key, grad_value]).reshape(2, block_count, -1, block_len, feat_width)
    extended = jnp.zeros((2, block_count + 2, block_len, feat_width), jnp.float32)
    for offset in range(3):
        extended = extended.at[:, offset : offset + block_count].add(key_grads[:, :, offset])
    from_right = from_behind(extended[:, :1].astype(jnp.bfloat16), "blk", -1).astype(jnp.float32)
    from_left = from_behind(extended[:, block_count + 1 :].astype(jnp.bfloat16), "blk", 1).astype(
        jnp.float32
    )
    own_grads = extended[:, 1 : block_count + 1]
    own_grads = own_grads.at[:, block_count - 1 :].add(from_right)
    own_grads = own_grads.at[:, :1].add(from_left)
    far_terms = jnp.transpose(key_grads[:, :, 3:], (0, 2, 1, 3, 4)).reshape(
        2, item_count, block_len, feat_width
    )
    padded = jnp.concatenate([far_terms, jnp.zeros_like(far_terms[:, :1])], axis=1)
    outgoing = jnp.take(padded, slot_item, axis=1)
    returned = lax.all_to_all(
        outgoing.astype(jnp.bfloat16), "slab", split_axis=1, concat_axis=1, tiled=True
    ).astype(outgoing.dtype)
    returned_terms = jnp.take(returned, item_slot, axis=1).reshape(
        2, 3, block_count, block_len, feat_width
    )
    own_grads = own_grads + jnp.sum(returned_terms, axis=1)
    grad_low = own_grads.reshape(2, rows_dev, feat_width).astype(jnp.bfloat16)
    query_low = grad_query.reshape(rows_dev, feat_width).astype(jnp.bfloat16)
    partial_sum = lax.dot_general(query_low, w_query, contract, preferred_element_type=jnp.float32)
    partial_sum = partial_sum + lax.dot_general(
        grad_low[0], w_key, contract, preferred_element_type=jnp.float32
    )
    partial_sum = partial_sum + lax.dot_general(
        grad_low[1], w_value, contract, preferred_element_type=jnp.float32
    )
    placed = jnp.zeros_like(partial_sum).at[node_order].set(partial_sum)
    head_share = lax.psum_scatter(
        placed.astype(jnp.bfloat16), "head", scatter_dimension=1, tiled=True
    )
    return head_share


def solution(mesh):
    in_specs = (
        P(("parts", "slab", "blk"), None),
        P(("parts", "slab", "blk"), None),
        P(None, "head"),
        P(None, "head"),
        P(None, "head"),
        P("head", None),
        P(("parts", "slab", "blk"), None),
        P(None, ("parts", "slab", "blk")),
        P(("parts", "slab", "blk")),
    )
    out_specs = P(("parts", "slab", "blk"), "head")
    return jax.shard_map(body, mesh=mesh, in_specs=in_specs, out_specs=out_specs, check_vma=False)
```

profile of v0, /device:TPU:0, one launch (start us, length us, event | category | flops | bytes accessed | tf_op | source)
XLA Modules:
  0.0 128.6 jit_solution(15643832790657309337)
XLA Ops:
  9.7 2.2 %gather_fusion.4 = bf16[256,512]{1,0:T(8,128)(2,1)S(1)} fusion(bf16[256,512]{1,0:T(8,128)(2,1)} %param.23, s32[1024]{0:T(1024)S(1)} %pad_clamp_fusion.3), kind=kCustom, calls=%fused_computation.clone | custom fusion | bytes 525312 | tf_op jit(solution)/shard_map/jit(_take)/gather | solution.py:78
  14.3 6.5 %all-to-all-start = ((bf16[2,8,128,256]{3,2,0,1:T(8,128)(2,1)}), bf16[2,8,128,256]{3,2,0,1:T(8,128)(2,1)S(1)}, u32[]{:S(2)}, u32[]{:S(2)}) async-start(bf16[2,8,128,256]{3,2,0,1:T(8,128)(2,1)} %select_bitcast_fusion), calls=%async_computation | async-start | bytes 2097152 | tf_op jit(solution)/shard_map/all_to_all | solution.py:105
  20.8 1.6 %collective-permute-start = (bf16[2,128,256]{2,1,0:T(8,128)(2,1)S(1)}, bf16[2,128,256]{2,1,0:T(8,128)(2,1)S(1)}, u32[]{:S(2)}, u32[]{:S(2)}) collective-permute-start(bf16[2,128,256]{2,1,0:T(8,128)(2,1)S(1)} %get-tuple-element.185), channel_id=1, source_target_pairs={{0,2},{2,0},{1,3},{3,1},{4,6},{6,4},{5,7},{7,5},{8,10},{10,8},{9,1... | collective-permute-start | bytes 393224 | tf_op jit(solution)/shard_map/ppermute | solution.py:16
  24.6 1.2 convolution_convert_fusion
  27.2 1.4 %collective-permute-done.1 = bf16[2,128,256]{2,1,0:T(8,128)(2,1)S(1)} collective-permute-done((bf16[2,128,256]{2,1,0:T(8,128)(2,1)S(1)}, bf16[2,128,256]{2,1,0:T(8,128)(2,1)S(1)}, u32[]{:S(2)}, u32[]{:S(2)}) %collective-permute-start.1) | collective-permute-done | bytes 131104 | tf_op jit(solution)/shard_map/ppermute | solution.py:17
  28.8 17.8 %all-to-all-done = bf16[2,8,128,256]{3,2,0,1:T(8,128)(2,1)S(1)} async-done(((bf16[2,8,128,256]{3,2,0,1:T(8,128)(2,1)}), bf16[2,8,128,256]{3,2,0,1:T(8,128)(2,1)S(1)}, u32[]{:S(2)}, u32[]{:S(2)}) %all-to-all-start) | async-done | bytes 1048608 | tf_op jit(solution)/shard_map/all_to_all | solution.py:105
  51.0 10.3 %while.19 = (s32[]{:T(128)}, bf16[2,1,128,4,64]{2,4,3,1,0:T(8,128)(2,1)S(1)}, f32[2,1,768,4,64]{2,4,3,1,0:T(8,128)}, f32[2,1,768,4,64]{2,4,3,1,0:T(8,128)}, bf16...) while((s32[]{:T(128)}, ...), condition=%wide.region_7.9_spmd, body=%wide.region_3.0_spmd.sunk | while | flops 307428352 | bytes 26441652 | solution.py:121
  59.7 1.2 fusion.105
  61.9 2.7 %stack.40 = f32[1,2,6,128,256]{3,2,4,1,0:T(8,128)} reshape(f32[2,1,768,4,64]{2,4,3,1,0:T(8,128)} %get-tuple-element.116) | data formatting | bytes 3145728 | tf_op jit(solution)/shard_map/stack | solution.py:133
  64.6 1.9 %copy.85 = f32[1,2,6,128,256]{4,3,1,0,2:T(8,128)S(1)} copy(f32[1,2,6,128,256]{3,2,4,1,0:T(8,128)} %stack.40) | data formatting | bytes 3145728 | tf_op jit(solution)/shard_map/stack | solution.py:133
  66.6 1.6 %stack.41 = f32[1,2,6,128,256]{3,2,4,1,0:T(8,128)} reshape(f32[2,1,768,4,64]{2,4,3,1,0:T(8,128)S(1)} %copy-done.4) | data formatting | bytes 3145728 | tf_op jit(solution)/shard_map/stack | solution.py:133
  68.2 1.8 %copy.86 = f32[1,2,6,128,256]{4,3,1,0,2:T(8,128)S(1)} copy(f32[1,2,6,128,256]{3,2,4,1,0:T(8,128)} %stack.41) | data formatting | bytes 3145728 | tf_op jit(solution)/shard_map/stack | solution.py:133
  71.3 2.8 %gather_fusion.2 = bf16[8,2,128,256]{3,2,1,0:T(8,128)(2,1)} fusion(bf16[2,7,128,256]{3,2,1,0:T(8,128)(2,1)} %concatenate.31, s32[1024]{0:T(1024)S(1)} %get-tuple-element.191), kind=kCustom, calls=%fused_computation.4 | custom fusion | bytes 2097184 | tf_op jit(solution)/shard_map/jit(_take)/gather | solution.py:148
  74.1 2.6 %fusion.34 = bf16[2,8,128,256]{3,2,0,1:T(8,128)(2,1)} fusion(bf16[8,2,128,256]{3,2,1,0:T(8,128)(2,1)} %gather_fusion.2, pred[8]{0:T(512)(128)(4,1)S(1)} %copy-done.11), kind=kLoop, calls=%fused_computation.60 | loop fusion | flops 524288 | bytes 2097160 | tf_op jit(solution)/shard_map/convert_element_type | solution.py:150
  76.7 4.3 %all-to-all-start.1 = ((bf16[2,8,128,256]{3,2,0,1:T(8,128)(2,1)}), bf16[2,8,128,256]{3,2,0,1:T(8,128)(2,1)}, u32[]{:S(2)}, u32[]{:S(2)}) async-start(bf16[2,8,128,256]{3,2,0,1:T(8,128)(2,1)} %fusion.34), calls=%async_computation.1 | async-start | bytes 2097152 | tf_op jit(solution)/shard_map/all_to_all | solution.py:149
  81.6 1.6 %collective-permute-start.2 = (bf16[2,1,128,256]{3,2,1,0:T(8,128)(2,1)S(1)}, bf16[2,1,128,256]{3,2,1,0:T(8,128)(2,1)S(1)}, u32[]{:S(2)}, u32[]{:S(2)}) collective-permute-start(bf16[2,1,128,256]{3,2,1,0:T(8,128)(2,1)S(1)} %slice.266), channel_id=1, source_target_pairs={{0,2},{2,0},{1,3},{3,1},{4,6},{6,4},{5,7},{7,5},{8,10},{10,8},{9,1... | collective-permute-start | bytes 393224 | tf_op jit(solution)/shard_map/ppermute | solution.py:25
  84.1 3.4 %collective-permute-done.2 = bf16[2,1,128,256]{3,2,1,0:T(8,128)(2,1)S(1)} collective-permute-done((bf16[2,1,128,256]{3,2,1,0:T(8,128)(2,1)S(1)}, bf16[2,1,128,256]{3,2,1,0:T(8,128)(2,1)S(1)}, u32[]{:S(2)}, u32[]{:S(2)}) %collective-permute-start.2) | collective-permute-done | bytes 131104 | tf_op jit(solution)/shard_map/ppermute | solution.py:25
  87.6 1.4 %collective-permute-done.3 = bf16[2,1,128,256]{3,2,1,0:T(8,128)(2,1)S(1)} collective-permute-done((bf16[2,1,128,256]{3,2,1,0:T(8,128)(2,1)S(1)}, bf16[2,1,128,256]{3,2,1,0:T(8,128)(2,1)S(1)}, u32[]{:S(2)}, u32[]{:S(2)}) %collective-permute-start.3) | collective-permute-done | bytes 131104 | tf_op jit(solution)/shard_map/ppermute | solution.py:25
  89.0 17.2 %all-to-all-done.1 = bf16[2,8,128,256]{3,2,0,1:T(8,128)(2,1)} async-done(((bf16[2,8,128,256]{3,2,0,1:T(8,128)(2,1)}), bf16[2,8,128,256]{3,2,0,1:T(8,128)(2,1)}, u32[]{:S(2)}, u32[]{:S(2)}) %all-to-all-start.1) | async-done | bytes 1048608 | tf_op jit(solution)/shard_map/all_to_all | solution.py:149
  106.2 1.4 %convert_element_type.78 = f32[2,8,128,256]{3,2,0,1:T(8,128)S(1)} convert(bf16[2,8,128,256]{3,2,0,1:T(8,128)(2,1)} %all-to-all-done.1) | non-fusion elementwise | flops 524288 | bytes 3145728 | tf_op jit(solution)/shard_map/convert_element_type | solution.py:151
  107.7 1.8 %gather_fusion.3 = f32[6,2,128,256]{3,2,1,0:T(8,128)} fusion(f32[2,8,128,256]{3,2,0,1:T(8,128)S(1)} %convert_element_type.78, s32[1024]{0:T(1024)S(1)} %pad_clamp_fusion.1), kind=kCustom, calls=%fused_computation.5 | custom fusion | bytes 3145752 | tf_op jit(solution)/shard_map/jit(_take)/gather | solution.py:152
  109.4 1.6 %copy.88 = f32[2,6,128,256]{3,2,1,0:T(8,128)S(1)} copy(f32[2,6,128,256]{3,2,0,1:T(8,128)} %bitcast.204) | data formatting | bytes 3145728 | tf_op jit(solution)/shard_map/jit(_take)/gather | solution.py:152
  112.5 1.6 %scatter_custom_fusion = f32[256,512]{1,0:T(8,128)S(1)} fusion(s32[256]{0:T(256)S(1)} %compare_select_fusion.1, f32[256,512]{1,0:T(8,128)S(1)} %convolution_add_fusion, f32[]{:T(128)} %constant.251.clone.1), kind=kCustom, calls=%fused_computation.87 | custom fusion | bytes 524292 | tf_op jit(solution)/shard_map/scatter | solution.py:165
  114.9 6.9 %reduce-scatter.2.cloned.1.call-done = bf16[256,256]{1,0:T(8,128)(2,1)} async-done(((bf16[256,512]{1,0:T(8,128)(2,1)}), bf16[256,256]{1,0:T(8,128)(2,1)}) %reduce-scatter.2.cloned.1.call-update) | async-done | bytes 131088 | tf_op jit(solution)/shard_map/reduce_scatter | solution.py:166
  (120 shorter events, 28.4 us)
Async XLA Ops:
  6.5 17.8 %copy-start = (bf16[512,256]{1,0:T(8,128)(2,1)S(1)}, bf16[512,256]{1,0:T(8,128)(2,1)}, u32[]{:S(2)}) copy-start(bf16[512,256]{1,0:T(8,128)(2,1)} %param.25) | copy-start | bytes 786436
  6.5 5.4 %copy-start.5 = (bf16[512,256]{1,0:T(8,128)(2,1)S(1)}, bf16[512,256]{1,0:T(8,128)(2,1)}, u32[]{:S(2)}) copy-start(bf16[512,256]{1,0:T(8,128)(2,1)} %param.26) | copy-start | bytes 786436
  9.7 2.5 %copy-start.7 = (bf16[512,256]{1,0:T(8,128)(2,1)S(1)}, bf16[512,256]{1,0:T(8,128)(2,1)}, u32[]{:S(2)}) copy-start(bf16[512,256]{1,0:T(8,128)(2,1)} %param.27) | copy-start | bytes 786436
  14.3 8.7 %copy-start.1 = (bf16[256,512]{1,0:T(8,128)(2,1)S(1)}, bf16[256,512]{1,0:T(8,128)(2,1)}, u32[]{:S(2)}) copy-start(bf16[256,512]{1,0:T(8,128)(2,1)} %param.24) | copy-start | bytes 786436
  14.3 32.2 %all-to-all-start = ((bf16[2,8,128,256]{3,2,0,1:T(8,128)(2,1)}), bf16[2,8,128,256]{3,2,0,1:T(8,128)(2,1)S(1)}, u32[]{:S(2)}, u32[]{:S(2)}) async-start(bf16[2,8,128,256]{3,2,0,1:T(8,128)(2,1)} %select_bitcast_fusion), calls=%async_computation | async-start | bytes 2097152 | tf_op jit(solution)/shard_map/all_to_all | solution.py:105
  20.8 3.4 %copy-start.12 = (s32[2,3]{1,0:T(2,128)S(1)}, s32[2,3]{1,0:T(2,128)}, u32[]{:S(2)}) copy-start(s32[2,3]{1,0:T(2,128)} %param.29) | copy-start | bytes 76
  20.8 6.4 %collective-permute-start = (bf16[2,128,256]{2,1,0:T(8,128)(2,1)S(1)}, bf16[2,128,256]{2,1,0:T(8,128)(2,1)S(1)}, u32[]{:S(2)}, u32[]{:S(2)}) collective-permute-start(bf16[2,128,256]{2,1,0:T(8,128)(2,1)S(1)} %get-tuple-element.185), channel_id=1, source_target_pairs={{0,2},{2,0},{1,3},{3,1},{4,6},{6,4},{5,7},{7,5},{8,10},{10,8},{9,1... | collective-permute-start | bytes 393224 | tf_op jit(solution)/shard_map/ppermute | solution.py:16
  22.4 6.3 %collective-permute-start.1 = (bf16[2,128,256]{2,1,0:T(8,128)(2,1)S(1)}, bf16[2,128,256]{2,1,0:T(8,128)(2,1)S(1)}, u32[]{:S(2)}, u32[]{:S(2)}) collective-permute-start(bf16[2,128,256]{2,1,0:T(8,128)(2,1)S(1)} %get-tuple-element.186), channel_id=1, source_target_pairs={{2,0},{0,2},{3,1},{1,3},{6,4},{4,6},{7,5},{5,7},{10,8},{8,10},{11,... | collective-permute-start | bytes 393224 | tf_op jit(solution)/shard_map/ppermute | solution.py:17
  51.1 1.4 %copy-start.2 = (f32[2,1,768,4,64]{2,4,3,1,0:T(8,128)S(1)}, f32[2,1,768,4,64]{2,4,3,1,0:T(8,128)}, u32[]{:S(2)}) copy-start(f32[2,1,768,4,64]{2,4,3,1,0:T(8,128)} %get-tuple-element.265) | copy-start | bytes 4718596 | tf_op jit(solution)/shard_map/while
  52.9 1.1 copy-start.3
  56.2 1.4 %copy-start.2 = (f32[2,1,768,4,64]{2,4,3,1,0:T(8,128)S(1)}, f32[2,1,768,4,64]{2,4,3,1,0:T(8,128)}, u32[]{:S(2)}) copy-start(f32[2,1,768,4,64]{2,4,3,1,0:T(8,128)} %get-tuple-element.265) | copy-start | bytes 4718596 | tf_op jit(solution)/shard_map/while
  58.1 1.1 copy-start.3
  61.3 0.7 copy-start.9
  64.6 2.0 %copy-start.4 = (f32[2,1,768,4,64]{2,4,3,1,0:T(8,128)S(1)}, f32[2,1,768,4,64]{2,4,3,1,0:T(8,128)}, u32[]{:S(2)}) copy-start(f32[2,1,768,4,64]{2,4,3,1,0:T(8,128)} %get-tuple-element.117) | copy-start | bytes 4718596
  70.2 3.8 %copy-start.11 = (pred[8]{0:T(512)(128)(4,1)S(1)}, pred[8]{0:T(512)(128)(4,1)}, u32[]{:S(2)}) copy-start(pred[8]{0:T(512)(128)(4,1)} %get-tuple-element.187) | copy-start | bytes 28
  76.7 29.5 %all-to-all-start.1 = ((bf16[2,8,128,256]{3,2,0,1:T(8,128)(2,1)}), bf16[2,8,128,256]{3,2,0,1:T(8,128)(2,1)}, u32[]{:S(2)}, u32[]{:S(2)}) async-start(bf16[2,8,128,256]{3,2,0,1:T(8,128)(2,1)} %fusion.34), calls=%async_computation.1 | async-start | bytes 2097152 | tf_op jit(solution)/shard_map/all_to_all | solution.py:149
  80.9 40.9 %reduce-scatter.2.cloned.1.call-start = ((), (), s32[]{:S(2)}) async-start(), calls=%async_computation.3 | async-start | bytes 393216 | tf_op jit(solution)/shard_map/reduce_scatter | solution.py:166
  81.5 2.2 %copy-start.10 = (bf16[2,1,128,4,64]{2,4,3,1,0:T(8,128)(2,1)S(1)}, bf16[2,1,128,4,64]{2,4,3,1,0:T(8,128)(2,1)}, u32[]{:S(2)}) copy-start(bf16[2,1,128,4,64]{2,4,3,1,0:T(8,128)(2,1)} %copy-done.9) | copy-start | bytes 393220
  81.6 5.9 %collective-permute-start.2 = (bf16[2,1,128,256]{3,2,1,0:T(8,128)(2,1)S(1)}, bf16[2,1,128,256]{3,2,1,0:T(8,128)(2,1)S(1)}, u32[]{:S(2)}, u32[]{:S(2)}) collective-permute-start(bf16[2,1,128,256]{3,2,1,0:T(8,128)(2,1)S(1)} %slice.266), channel_id=1, source_target_pairs={{0,2},{2,0},{1,3},{3,1},{4,6},{6,4},{5,7},{7,5},{8,10},{10,8},{9,1... | collective-permute-start | bytes 393224 | tf_op jit(solution)/shard_map/ppermute | solution.py:25
  83.2 5.8 %collective-permute-start.3 = (bf16[2,1,128,256]{3,2,1,0:T(8,128)(2,1)S(1)}, bf16[2,1,128,256]{3,2,1,0:T(8,128)(2,1)S(1)}, u32[]{:S(2)}, u32[]{:S(2)}) collective-permute-start(bf16[2,1,128,256]{3,2,1,0:T(8,128)(2,1)S(1)} %slice.265), channel_id=1, source_target_pairs={{0,2},{2,0},{1,3},{3,1},{4,6},{6,4},{5,7},{7,5},{8,10},{10,8},{9,1... | collective-permute-start | bytes 393224 | tf_op jit(solution)/shard_map/ppermute | solution.py:25
  111.0 1.0 copy-start.6
  111.2 1.0 copy-start.8
Sparse Core Ops, SparseCore 0:
  115.0 6.7 reduce-scatter.1
where the time goes:
time: 129 us
  waiting for transfers between devices  48.8 us (38%)
  local copies, waits for them, and re-layouts  30.6 us (24%)
  starting transfers between devices  15.1 us (12%)
  between operations  13.9 us (11%)
  other arithmetic  10.2 us (8%)
  matrix products  9.91 us (8%)
    all_to_all x1, waiting for transfers between devices, body(): lax.all_to_all(sent_slots, 'slab', split_axis=1, concat_axis=1, tiled=True)  17.8 us
    all_to_all x1, waiting for transfers between devices, body(): lax.all_to_all(outgoing.astype(jnp.bfloat16), 'slab', split_axis=1, conca...  17.2 us
    another operation x4, local copies, waits for them, and re-layouts, body(): jnp.stack([grad_key, grad_value])  8.01 us
    reduce_scatter x1, waiting for transfers between devices, body(): lax.psum_scatter(placed.astype(jnp.bfloat16), 'head', scatter_dimension=1...  6.94 us
    all_to_all x1, starting transfers between devices, body(): lax.all_to_all(sent_slots, 'slab', split_axis=1, concat_axis=1, tiled=True)  6.45 us
    ppermute x2, waiting for transfers between devices, from_behind(): return lax.ppermute(value, axis, pairs)  4.81 us
    all_to_all x1, starting transfers between devices, body(): lax.all_to_all(outgoing.astype(jnp.bfloat16), 'slab', split_axis=1, conca...  4.25 us
    gather x2, local copies, waits for them, and re-layouts, body(): jnp.take(returned, item_slot, axis=1)  3.38 us
  transfers between devices with their start and end apart: 7, of which 7 were waited for; matrix products, arithmetic and copies ran while one was open for 4% of the time, Pallas kernels for 0%

commit v1 on v0

--- a/solution.py
+++ b/solution.py
@@ -4,6 +4,22 @@
 from jax.sharding import PartitionSpec as P
 
 HEAD_DIM = 64
+
+
+def swapped_with_each(x, axis, split, join):
+    ways, here = (lax.axis_size(axis), lax.axis_index(axis))
+    width = x.shape[split] // ways
+    dims = list(x.shape)
+    dims[split] = width
+    height = dims[join]
+    dims[join] = height * ways
+    full = jnp.zeros(dims, x.dtype)
+    for mask in range(ways):
+        part = lax.dynamic_slice_in_dim(x, (here ^ mask) * width, width, axis=split)
+        if mask:
+            part = lax.ppermute(part, axis, [(d, d ^ mask) for d in range(ways)])
+        full = lax.dynamic_update_slice_in_dim(full, part, (here ^ mask) * height, axis=join)
+    return full
 
 
 def padded_2(shard, sides, width):
@@ -146,9 +162,7 @@
     )
     padded = jnp.concatenate([far_terms, jnp.zeros_like(far_terms[:, :1])], axis=1)
     outgoing = jnp.take(padded, slot_item, axis=1)
-    returned = lax.all_to_all(
-        outgoing.astype(jnp.bfloat16), "slab", split_axis=1, concat_axis=1, tiled=True
-    ).astype(outgoing.dtype)
+    returned = swapped_with_each(outgoing.astype(jnp.bfloat16), "slab", 1, 1).astype(outgoing.dtype)
     returned_terms = jnp.take(returned, item_slot, axis=1).reshape(
         2, 3, block_count, block_len, feat_width
     )

time: 129 us -> 118 us (0.915)
  waiting for transfers between devices: 48.8 us -> 44.9 us
  other arithmetic: 10.2 us -> 6.8 us
  local copies, waits for them, and re-layouts: 30.6 us -> 28 us
    all_to_all x1 -> x0, waiting for transfers between devices: 17.2 us -> none  [body(): lax.all_to_all(outgoing.astype(jnp.bfloat16), 'slab', split_axis=1, conca...]
    ppermute x0 -> x3, waiting for transfers between devices: none -> 10.5 us  [swapped_with_each(): part = lax.ppermute(part, axis, [(d, d ^ mask) for d in range(ways)])]
    ppermute x0 -> x3, starting transfers between devices: none -> 4.44 us  [swapped_with_each(): part = lax.ppermute(part, axis, [(d, d ^ mask) for d in range(ways)])]
    all_to_all x1 -> x0, starting transfers between devices: 4.25 us -> none  [body(): lax.all_to_all(outgoing.astype(jnp.bfloat16), 'slab', split_axis=1, conca...]
    reduce_scatter x1, waiting for transfers between devices: 6.94 us -> 9.74 us  [body(): lax.psum_scatter(placed.astype(jnp.bfloat16), 'head', scatter_dimension=1...]
    convert_element_type x1, other arithmetic: 2.6 us -> 0.41 us  [body(): outgoing.astype(jnp.bfloat16)]
    gather x1, local copies, waits for them, and re-layouts: 2.75 us -> 0.61 us  [body(): outgoing = jnp.take(padded, slot_item, axis=1)]
  transfers between devices with their start and end apart: 7 -> 9, of which waited for: 7 -> 8; matrix products, arithmetic and copies ran while one was open for 4% -> 3% of each run, Pallas kernels for 0% -> 0%
where the time goes in v1:
time: 118 us
  waiting for transfers between devices  44.9 us (38%)
  local copies, waits for them, and re-layouts  28 us (24%)
  starting transfers between devices  15 us (13%)
  between operations  14 us (12%)
  matrix products  8.97 us (8%)
  other arithmetic  6.8 us (6%)
    all_to_all x1, waiting for transfers between devices, body(): lax.all_to_all(sent_slots, 'slab', split_axis=1, concat_axis=1, tiled=True)  17.8 us
    ppermute x3, waiting for transfers between devices, swapped_with_each(): part = lax.ppermute(part, axis, [(d, d ^ mask) for d in range(ways)])  10.5 us
    reduce_scatter x1, waiting for transfers between devices, body(): lax.psum_scatter(placed.astype(jnp.bfloat16), 'head', scatter_dimension=1...  9.74 us
    another operation x4, local copies, waits for them, and re-layouts, body(): jnp.stack([grad_key, grad_value])  8 us
    all_to_all x1, starting transfers between devices, body(): lax.all_to_all(sent_slots, 'slab', split_axis=1, concat_axis=1, tiled=True)  6.45 us
    ppermute x3, starting transfers between devices, swapped_with_each(): part = lax.ppermute(part, axis, [(d, d ^ mask) for d in range(ways)])  4.44 us
    ppermute x2, waiting for transfers between devices, from_behind(): return lax.ppermute(value, axis, pairs)  3.85 us
    gather x2, local copies, waits for them, and re-layouts, body(): jnp.take(returned, item_slot, axis=1)  3.4 us
  transfers between devices with their start and end apart: 9, of which 8 were waited for; matrix products, arithmetic and copies ran while one was open for 3% of the time, Pallas kernels for 0%

profile of v1, /device:TPU:0, one launch (start us, length us, event | category | flops | bytes accessed | tf_op | source)
XLA Modules:
  0.0 117.8 jit_solution(211933010456176238)
XLA Ops:
  9.7 2.2 %gather_fusion.4 = bf16[256,512]{1,0:T(8,128)(2,1)S(1)} fusion(bf16[256,512]{1,0:T(8,128)(2,1)} %param.23, s32[1024]{0:T(1024)S(1)} %pad_clamp_fusion.3), kind=kCustom, calls=%fused_computation.clone | custom fusion | bytes 525312 | tf_op jit(solution)/shard_map/jit(_take)/gather | solution.py:94
  14.4 6.5 %all-to-all-start = ((bf16[2,8,128,256]{3,2,0,1:T(8,128)(2,1)}), bf16[2,8,128,256]{3,2,0,1:T(8,128)(2,1)S(1)}, u32[]{:S(2)}, u32[]{:S(2)}) async-start(bf16[2,8,128,256]{3,2,0,1:T(8,128)(2,1)} %select_bitcast_fusion), calls=%async_computation | async-start | bytes 2097152 | tf_op jit(solution)/shard_map/all_to_all | solution.py:121
  20.9 1.6 %collective-permute-start = (bf16[2,128,256]{2,1,0:T(8,128)(2,1)S(1)}, bf16[2,128,256]{2,1,0:T(8,128)(2,1)S(1)}, u32[]{:S(2)}, u32[]{:S(2)}) collective-permute-start(bf16[2,128,256]{2,1,0:T(8,128)(2,1)S(1)} %get-tuple-element.198), channel_id=1, source_target_pairs={{0,2},{2,0},{1,3},{3,1},{4,6},{6,4},{5,7},{7,5},{8,10},{10,8},{9,1... | collective-permute-start | bytes 393224 | tf_op jit(solution)/shard_map/ppermute | solution.py:32
  25.7 1.6 %collective-permute-done = bf16[2,128,256]{2,1,0:T(8,128)(2,1)S(1)} collective-permute-done((bf16[2,128,256]{2,1,0:T(8,128)(2,1)S(1)}, bf16[2,128,256]{2,1,0:T(8,128)(2,1)S(1)}, u32[]{:S(2)}, u32[]{:S(2)}) %collective-permute-start) | collective-permute-done | bytes 131104 | tf_op jit(solution)/shard_map/ppermute | solution.py:32
  27.3 1.4 %collective-permute-done.1 = bf16[2,128,256]{2,1,0:T(8,128)(2,1)S(1)} collective-permute-done((bf16[2,128,256]{2,1,0:T(8,128)(2,1)S(1)}, bf16[2,128,256]{2,1,0:T(8,128)(2,1)S(1)}, u32[]{:S(2)}, u32[]{:S(2)}) %collective-permute-start.1) | collective-permute-done | bytes 131104 | tf_op jit(solution)/shard_map/ppermute | solution.py:33
  28.8 17.8 %all-to-all-done = bf16[2,8,128,256]{3,2,0,1:T(8,128)(2,1)S(1)} async-done(((bf16[2,8,128,256]{3,2,0,1:T(8,128)(2,1)}), bf16[2,8,128,256]{3,2,0,1:T(8,128)(2,1)S(1)}, u32[]{:S(2)}, u32[]{:S(2)}) %all-to-all-start) | async-done | bytes 1048608 | tf_op jit(solution)/shard_map/all_to_all | solution.py:121
  51.2 10.4 %while.19 = (s32[]{:T(128)}, bf16[2,1,128,4,64]{2,4,3,1,0:T(8,128)(2,1)S(1)}, f32[2,1,768,4,64]{2,4,3,1,0:T(8,128)}, f32[2,1,768,4,64]{2,4,3,1,0:T(8,128)}, bf16...) while((s32[]{:T(128)}, ...), condition=%wide.region_7.9_spmd, body=%wide.region_3.0_spmd.sunk | while | flops 307428352 | bytes 26441652 | solution.py:137
  54.8 1.2 fusion.104
  60.0 1.2 fusion.104
  61.5 2.7 %stack.40 = f32[1,2,6,128,256]{3,2,4,1,0:T(8,128)} reshape(f32[2,1,768,4,64]{2,4,3,1,0:T(8,128)} %get-tuple-element.116) | data formatting | bytes 3145728 | tf_op jit(solution)/shard_map/stack | solution.py:149
  64.2 1.9 %copy.115 = f32[1,2,6,128,256]{4,3,1,0,2:T(8,128)S(1)} copy(f32[1,2,6,128,256]{3,2,4,1,0:T(8,128)} %stack.40) | data formatting | bytes 3145728 | tf_op jit(solution)/shard_map/stack | solution.py:149
  66.2 1.6 %stack.41 = f32[1,2,6,128,256]{3,2,4,1,0:T(8,128)} reshape(f32[2,1,768,4,64]{2,4,3,1,0:T(8,128)S(1)} %copy-done.6) | data formatting | bytes 3145728 | tf_op jit(solution)/shard_map/stack | solution.py:149
  67.8 1.8 %copy.116 = f32[1,2,6,128,256]{4,3,1,0,2:T(8,128)S(1)} copy(f32[1,2,6,128,256]{3,2,4,1,0:T(8,128)} %stack.41) | data formatting | bytes 3145728 | tf_op jit(solution)/shard_map/stack | solution.py:149
  72.3 2.0 %collective-permute-start.5 = (bf16[2,2,128,256]{3,2,0,1:T(8,128)(2,1)S(1)}, bf16[2,2,128,256]{3,2,0,1:T(8,128)(2,1)S(1)}, u32[]{:S(2)}, u32[]{:S(2)}) collective-permute-start(bf16[2,2,128,256]{3,2,0,1:T(8,128)(2,1)S(1)} %get-tuple-element.190), channel_id=1, source_target_pairs={{0,8},{4,12},{8,0},{12,4},{1,9},{5,13},{9,1},{13,5},{2,10},{6,14},... | collective-permute-start | bytes 786440 | tf_op jit(solution)/shard_map/ppermute | solution.py:20
  74.3 2.4 %collective-permute-start.6 = (bf16[2,2,128,256]{3,2,0,1:T(8,128)(2,1)S(1)}, bf16[2,2,128,256]{3,2,0,1:T(8,128)(2,1)S(1)}, u32[]{:S(2)}, u32[]{:S(2)}) collective-permute-start(bf16[2,2,128,256]{3,2,0,1:T(8,128)(2,1)S(1)} %get-tuple-element.189), channel_id=1, source_target_pairs={{0,12},{4,8},{8,4},{12,0},{1,13},{5,9},{9,5},{13,1},{2,14},{6,10},... | collective-permute-start | bytes 786440 | tf_op jit(solution)/shard_map/ppermute | solution.py:20
  76.7 1.5 %collective-permute-start.2 = (bf16[2,1,128,256]{3,2,1,0:T(8,128)(2,1)S(1)}, bf16[2,1,128,256]{3,2,1,0:T(8,128)(2,1)S(1)}, u32[]{:S(2)}, u32[]{:S(2)}) collective-permute-start(bf16[2,1,128,256]{3,2,1,0:T(8,128)(2,1)S(1)} %slice.266), channel_id=1, source_target_pairs={{0,2},{2,0},{1,3},{3,1},{4,6},{6,4},{5,7},{7,5},{8,10},{10,8},{9,1... | collective-permute-start | bytes 393224 | tf_op jit(solution)/shard_map/ppermute | solution.py:41
  79.2 2.4 %collective-permute-done.2 = bf16[2,1,128,256]{3,2,1,0:T(8,128)(2,1)S(1)} collective-permute-done((bf16[2,1,128,256]{3,2,1,0:T(8,128)(2,1)S(1)}, bf16[2,1,128,256]{3,2,1,0:T(8,128)(2,1)S(1)}, u32[]{:S(2)}, u32[]{:S(2)}) %collective-permute-start.2) | collective-permute-done | bytes 131104 | tf_op jit(solution)/shard_map/ppermute | solution.py:41
  81.7 1.4 %collective-permute-done.3 = bf16[2,1,128,256]{3,2,1,0:T(8,128)(2,1)S(1)} collective-permute-done((bf16[2,1,128,256]{3,2,1,0:T(8,128)(2,1)S(1)}, bf16[2,1,128,256]{3,2,1,0:T(8,128)(2,1)S(1)}, u32[]{:S(2)}, u32[]{:S(2)}) %collective-permute-start.3) | collective-permute-done | bytes 131104 | tf_op jit(solution)/shard_map/ppermute | solution.py:41
  83.2 1.2 %collective-permute-done.4 = bf16[2,2,128,256]{3,2,0,1:T(8,128)(2,1)S(1)} collective-permute-done((bf16[2,2,128,256]{3,2,0,1:T(8,128)(2,1)S(1)}, bf16[2,2,128,256]{3,2,0,1:T(8,128)(2,1)S(1)}, u32[]{:S(2)}, u32[]{:S(2)}) %collective-permute-start.4) | collective-permute-done | bytes 262176 | tf_op jit(solution)/shard_map/ppermute | solution.py:20
  84.4 9.3 %collective-permute-done.5 = bf16[2,2,128,256]{3,2,0,1:T(8,128)(2,1)S(1)} collective-permute-done((bf16[2,2,128,256]{3,2,0,1:T(8,128)(2,1)S(1)}, bf16[2,2,128,256]{3,2,0,1:T(8,128)(2,1)S(1)}, u32[]{:S(2)}, u32[]{:S(2)}) %collective-permute-start.5) | collective-permute-done | bytes 262176 | tf_op jit(solution)/shard_map/ppermute | solution.py:20
  94.0 1.8 %gather_fusion.3 = f32[6,2,128,256]{3,2,1,0:T(8,128)} fusion(f32[2,8,128,256]{3,2,1,0:T(8,128)S(1)} %convert_element_type.78, s32[1024]{0:T(1024)S(1)} %pad_clamp_fusion.1), kind=kCustom, calls=%fused_computation.5 | custom fusion | bytes 3145752 | tf_op jit(solution)/shard_map/jit(_take)/gather | solution.py:166
  95.8 1.6 %copy.122 = f32[2,6,128,256]{3,2,1,0:T(8,128)S(1)} copy(f32[2,6,128,256]{3,2,0,1:T(8,128)} %bitcast.210) | data formatting | bytes 3145728 | tf_op jit(solution)/shard_map/jit(_take)/gather | solution.py:166
  98.9 1.6 %scatter_custom_fusion = f32[256,512]{1,0:T(8,128)S(1)} fusion(s32[256]{0:T(256)S(1)} %compare_select_fusion.1, f32[256,512]{1,0:T(8,128)S(1)} %convolution_add_fusion, f32[]{:T(128)} %constant.258.clone.1), kind=kCustom, calls=%fused_computation.94 | custom fusion | bytes 524292 | tf_op jit(solution)/shard_map/scatter | solution.py:179
  101.2 9.7 %reduce-scatter.2.cloned.1.call-done = bf16[256,256]{1,0:T(8,128)(2,1)} async-done(((bf16[256,512]{1,0:T(8,128)(2,1)}), bf16[256,256]{1,0:T(8,128)(2,1)}) %reduce-scatter.2.cloned.1.call-update) | async-done | bytes 131088 | tf_op jit(solution)/shard_map/reduce_scatter | solution.py:180
  (132 shorter events, 27.4 us)
Async XLA Ops:
  6.5 17.8 %copy-start = (bf16[512,256]{1,0:T(8,128)(2,1)S(1)}, bf16[512,256]{1,0:T(8,128)(2,1)}, u32[]{:S(2)}) copy-start(bf16[512,256]{1,0:T(8,128)(2,1)} %param.25) | copy-start | bytes 786436
  6.5 5.5 %copy-start.7 = (bf16[512,256]{1,0:T(8,128)(2,1)S(1)}, bf16[512,256]{1,0:T(8,128)(2,1)}, u32[]{:S(2)}) copy-start(bf16[512,256]{1,0:T(8,128)(2,1)} %param.26) | copy-start | bytes 786436
  9.7 2.5 %copy-start.9 = (bf16[512,256]{1,0:T(8,128)(2,1)S(1)}, bf16[512,256]{1,0:T(8,128)(2,1)}, u32[]{:S(2)}) copy-start(bf16[512,256]{1,0:T(8,128)(2,1)} %param.27) | copy-start | bytes 786436
  14.4 8.7 %copy-start.1 = (bf16[256,512]{1,0:T(8,128)(2,1)S(1)}, bf16[256,512]{1,0:T(8,128)(2,1)}, u32[]{:S(2)}) copy-start(bf16[256,512]{1,0:T(8,128)(2,1)} %param.24) | copy-start | bytes 786436
  14.4 32.2 %all-to-all-start = ((bf16[2,8,128,256]{3,2,0,1:T(8,128)(2,1)}), bf16[2,8,128,256]{3,2,0,1:T(8,128)(2,1)S(1)}, u32[]{:S(2)}, u32[]{:S(2)}) async-start(bf16[2,8,128,256]{3,2,0,1:T(8,128)(2,1)} %select_bitcast_fusion), calls=%async_computation | async-start | bytes 2097152 | tf_op jit(solution)/shard_map/all_to_all | solution.py:121
  20.8 3.5 %copy-start.13 = (s32[2,3]{1,0:T(2,128)S(1)}, s32[2,3]{1,0:T(2,128)}, u32[]{:S(2)}) copy-start(s32[2,3]{1,0:T(2,128)} %param.29) | copy-start | bytes 76
  20.8 90.1 %reduce-scatter.2.cloned.1.call-start = ((), (), s32[]{:S(2)}) async-start(), calls=%async_computation.2 | async-start | bytes 393216 | tf_op jit(solution)/shard_map/reduce_scatter | solution.py:180
  20.9 6.4 %collective-permute-start = (bf16[2,128,256]{2,1,0:T(8,128)(2,1)S(1)}, bf16[2,128,256]{2,1,0:T(8,128)(2,1)S(1)}, u32[]{:S(2)}, u32[]{:S(2)}) collective-permute-start(bf16[2,128,256]{2,1,0:T(8,128)(2,1)S(1)} %get-tuple-element.198), channel_id=1, source_target_pairs={{0,2},{2,0},{1,3},{3,1},{4,6},{6,4},{5,7},{7,5},{8,10},{10,8},{9,1... | collective-permute-start | bytes 393224 | tf_op jit(solution)/shard_map/ppermute | solution.py:32
  22.4 6.3 %collective-permute-start.1 = (bf16[2,128,256]{2,1,0:T(8,128)(2,1)S(1)}, bf16[2,128,256]{2,1,0:T(8,128)(2,1)S(1)}, u32[]{:S(2)}, u32[]{:S(2)}) collective-permute-start(bf16[2,128,256]{2,1,0:T(8,128)(2,1)S(1)} %get-tuple-element.199), channel_id=1, source_target_pairs={{2,0},{0,2},{3,1},{1,3},{6,4},{4,6},{7,5},{5,7},{10,8},{8,10},{11,... | collective-permute-start | bytes 393224 | tf_op jit(solution)/shard_map/ppermute | solution.py:33
  23.1 1.5 %copy-start.12 = (bf16[256,512]{1,0:T(8,128)(2,1)S(1)}, bf16[256,512]{1,0:T(8,128)(2,1)}, u32[]{:S(2)}) copy-start(bf16[256,512]{1,0:T(8,128)(2,1)} %param.28) | copy-start | bytes 786436
  51.3 1.4 %copy-start.4 = (f32[2,1,768,4,64]{2,4,3,1,0:T(8,128)S(1)}, f32[2,1,768,4,64]{2,4,3,1,0:T(8,128)}, u32[]{:S(2)}) copy-start(f32[2,1,768,4,64]{2,4,3,1,0:T(8,128)} %get-tuple-element.278) | copy-start | bytes 4718596 | tf_op jit(solution)/shard_map/while
  53.1 1.2 copy-start.5
  56.5 1.4 %copy-start.4 = (f32[2,1,768,4,64]{2,4,3,1,0:T(8,128)S(1)}, f32[2,1,768,4,64]{2,4,3,1,0:T(8,128)}, u32[]{:S(2)}) copy-start(f32[2,1,768,4,64]{2,4,3,1,0:T(8,128)} %get-tuple-element.278) | copy-start | bytes 4718596 | tf_op jit(solution)/shard_map/while
  58.3 1.2 copy-start.5
  64.2 2.0 %copy-start.6 = (f32[2,1,768,4,64]{2,4,3,1,0:T(8,128)S(1)}, f32[2,1,768,4,64]{2,4,3,1,0:T(8,128)}, u32[]{:S(2)}) copy-start(f32[2,1,768,4,64]{2,4,3,1,0:T(8,128)} %get-tuple-element.117) | copy-start | bytes 4718596
  70.1 0.8 copy-start.2
  72.2 9.5 %copy-start.3 = (f32[2,2,128,256]{3,2,1,0:T(8,128)S(1)}, f32[2,2,128,256]{3,2,1,0:T(8,128)}, u32[]{:S(2)}) copy-start(f32[2,2,128,256]{3,2,1,0:T(8,128)} %copy-done.2) | copy-start | bytes 1572868
  72.2 12.2 %collective-permute-start.4 = (bf16[2,2,128,256]{3,2,0,1:T(8,128)(2,1)S(1)}, bf16[2,2,128,256]{3,2,0,1:T(8,128)(2,1)S(1)}, u32[]{:S(2)}, u32[]{:S(2)}) collective-permute-start(bf16[2,2,128,256]{3,2,0,1:T(8,128)(2,1)S(1)} %get-tuple-element.191), channel_id=1, source_target_pairs={{0,4},{4,0},{8,12},{12,8},{1,5},{5,1},{9,13},{13,9},{2,6},{6,2},{1... | collective-permute-start | bytes 786440 | tf_op jit(solution)/shard_map/ppermute | solution.py:20
  72.3 21.4 %collective-permute-start.5 = (bf16[2,2,128,256]{3,2,0,1:T(8,128)(2,1)S(1)}, bf16[2,2,128,256]{3,2,0,1:T(8,128)(2,1)S(1)}, u32[]{:S(2)}, u32[]{:S(2)}) collective-permute-start(bf16[2,2,128,256]{3,2,0,1:T(8,128)(2,1)S(1)} %get-tuple-element.190), channel_id=1, source_target_pairs={{0,8},{4,12},{8,0},{12,4},{1,9},{5,13},{9,1},{13,5},{2,10},{6,14},... | collective-permute-start | bytes 786440 | tf_op jit(solution)/shard_map/ppermute | solution.py:20
  74.3 19.4 %collective-permute-start.6 = (bf16[2,2,128,256]{3,2,0,1:T(8,128)(2,1)S(1)}, bf16[2,2,128,256]{3,2,0,1:T(8,128)(2,1)S(1)}, u32[]{:S(2)}, u32[]{:S(2)}) collective-permute-start(bf16[2,2,128,256]{3,2,0,1:T(8,128)(2,1)S(1)} %get-tuple-element.189), channel_id=1, source_target_pairs={{0,12},{4,8},{8,4},{12,0},{1,13},{5,9},{9,5},{13,1},{2,14},{6,10},... | collective-permute-start | bytes 786440 | tf_op jit(solution)/shard_map/ppermute | solution.py:20
  76.7 5.0 %collective-permute-start.2 = (bf16[2,1,128,256]{3,2,1,0:T(8,128)(2,1)S(1)}, bf16[2,1,128,256]{3,2,1,0:T(8,128)(2,1)S(1)}, u32[]{:S(2)}, u32[]{:S(2)}) collective-permute-start(bf16[2,1,128,256]{3,2,1,0:T(8,128)(2,1)S(1)} %slice.266), channel_id=1, source_target_pairs={{0,2},{2,0},{1,3},{3,1},{4,6},{6,4},{5,7},{7,5},{8,10},{10,8},{9,1... | collective-permute-start | bytes 393224 | tf_op jit(solution)/shard_map/ppermute | solution.py:41
  78.1 5.0 %collective-permute-start.3 = (bf16[2,1,128,256]{3,2,1,0:T(8,128)(2,1)S(1)}, bf16[2,1,128,256]{3,2,1,0:T(8,128)(2,1)S(1)}, u32[]{:S(2)}, u32[]{:S(2)}) collective-permute-start(bf16[2,1,128,256]{3,2,1,0:T(8,128)(2,1)S(1)} %slice.265), channel_id=1, source_target_pairs={{0,2},{2,0},{1,3},{3,1},{4,6},{6,4},{5,7},{7,5},{8,10},{10,8},{9,1... | collective-permute-start | bytes 393224 | tf_op jit(solution)/shard_map/ppermute | solution.py:41
  97.4 1.0 copy-start.8
  97.6 1.0 copy-start.10
  (1 other events, 0.7 us)
Sparse Core Ops, SparseCore 0:
  101.3 9.5 reduce-scatter.1
